TPU v7x, 256 devices: a whole 4x4x8 slice. The times are simulated.
256 devices in a mesh: seq: 64 (over y, z, core), mp: 4 (over x).
Axes of the slice: x: 4, y: 4, z: 8, core: 2. Of those that a mesh axis runs over, the one named last changes fastest.
Arguments:
- tokens: bfloat16 [8192, 3584], P('seq'), may hold values from -6 to 6
- query_weight: bfloat16 [3584, 4096], P('seq', 'mp'), may hold values from -0.09375 to 0.09375
- key_weight: bfloat16 [3584, 4096], P('seq', 'mp'), may hold values from -0.09375 to 0.09375
- value_weight: bfloat16 [3584, 4096], P('seq', 'mp'), may hold values from -0.09375 to 0.09375
- adapter_down_maps: bfloat16 [3584, 128], replicated, may hold values from -0.09375 to 0.09375
- lifting_matrices: bfloat16 [2, 64, 4096], P(None, None, 'mp'), may hold values from -0.75 to 0.75
- decay_logarithms: float32 [32, 8192], P('mp', 'seq'), may hold values from -1 to 0, as said below
- output_gradient: bfloat16 [8192, 4096], P('seq', 'mp'), may hold values from -0.06591797 to 0.06591797
Outputs:
- grad_down: float32 [3584, 128], P(('seq', 'mp'))
- grad_up: float32 [2, 64, 4096], P(None, None, 'mp')
Inputs may be any that keep to these rules, and one draw needn't show every extreme that they name: `decay_logarithms`: every entry is negative.
All inputs are finite; a program needn't handle non-finite values.
Results may differ from a plain program's by a relative error of at most 0.006.
Values may be sent and summed in bfloat16 or wider, within the bound.
No kernel may reach another device: no remote copies, remote signals or barrier semaphores. Data moves between devices by JAX's collectives and lax.ppermute only.
A program may use at most 192 MiB of HBM per device.

v0:
```python
import jax
import jax.numpy as jnp
from jax import lax
from jax.sharding import PartitionSpec as P

adapter_scale = 2.0
eps_norm = 1e-06
exact_arithmetic = lax.Precision.HIGHEST


def carried_in(value, axis, join, neutral, backward):
    count, mine = (lax.axis_size(axis), lax.axis_index(axis))
    pieces = jax.tree.map(lambda part: lax.all_gather(part, axis), value)
    if backward:
        pieces = jax.tree.map(lambda part: part[::-1], pieces)
        mine = count - 1 - mine
    so_far = jax.tree.map(
        lambda part, zero: jnp.full_like(part, 0) + jnp.asarray(zero, part.dtype), value, neutral
    )

    def hop(position, so_far):
        longer = join(so_far, jax.tree.map(lambda part: part[position], pieces))
        return jax.tree.map(lambda new, old: jnp.where(position < mine, new, old), longer, so_far)

    return lax.fori_loop(0, count - 1, hop, so_far)


def combine(earlier, later):
    return (earlier[0] * later[0], later[0][:, None, None] * earlier[1] + later[1])


def split_heads(flat, heads):
    return flat.reshape(flat.shape[0], heads, flat.shape[1] // heads).transpose(1, 0, 2)


def join_heads(arr):
    return arr.transpose(1, 0, 2).reshape(arr.shape[1], arr.shape[0] * arr.shape[2])


def on_device(
    tokens,
    query_weight,
    key_weight,
    value_weight,
    adapter_down_maps,
    lifting_matrices,
    decay_logarithms,
    output_gradient,
):
    length = tokens.shape[0]
    heads = decay_logarithms.shape[0]
    rank_index = lifting_matrices.shape[1]
    low_product = jnp.dot(tokens, adapter_down_maps, preferred_element_type=jnp.float32).astype(
        jnp.bfloat16
    )
    query_low_product = low_product[:, :rank_index]
    value_low_product = low_product[:, rank_index:]
    cumulative = jnp.cumsum(decay_logarithms, axis=1)
    total = cumulative[:, -1]
    gain = jnp.exp(total)
    tail = jnp.exp(total[:, None] - cumulative)
    lead = jnp.exp(cumulative)
    causal = jnp.arange(length)[:, None] >= jnp.arange(length)[None, :]
    spread = cumulative[:, :, None] - cumulative[:, None, :]
    decay_mat = jnp.where(causal[None], jnp.exp(jnp.where(causal[None], spread, 0.0)), 0.0)
    pieces = (
        lax.all_gather(query_weight, "seq", axis=0, tiled=True),
        lax.all_gather(key_weight, "seq", axis=0, tiled=True),
        lax.all_gather(value_weight, "seq", axis=0, tiled=True),
    )
    columns = tokens
    query_frozen_part, key_base, value_frozen_part = tuple(
        (jnp.dot(columns, piece, preferred_element_type=jnp.float32) for piece in pieces)
    )
    value_before_norm = value_frozen_part + adapter_scale * jnp.dot(
        value_low_product, lifting_matrices[1], preferred_element_type=jnp.float32
    )
    key_heads = split_heads(jax.nn.silu(key_base).astype(jnp.bfloat16), heads)
    value_heads = split_heads(value_before_norm.astype(jnp.bfloat16), heads)
    key_f = key_heads.astype(jnp.float32)
    local = jnp.einsum(
        "hsi,hsj->hij",
        key_f * tail[:, :, None],
        value_heads.astype(jnp.float32),
        precision=exact_arithmetic,
    )
    state_in = carried_in(
        (gain, local), "seq", combine, (jnp.ones_like(gain), jnp.zeros_like(local)), False
    )[1]
    key_heads, key_f, value_heads, state_in = (key_heads, key_f, value_heads, state_in)
    query_before_norm = query_frozen_part + adapter_scale * jnp.dot(
        query_low_product, lifting_matrices[0], preferred_element_type=jnp.float32
    )
    query_heads = split_heads(jax.nn.silu(query_before_norm).astype(jnp.bfloat16), heads)
    query_f = query_heads.astype(jnp.float32)
    scores = jnp.einsum("htd,hsd->hts", query_heads, key_heads, preferred_element_type=jnp.float32)
    mixed = (scores * decay_mat).astype(jnp.bfloat16)
    attn = jnp.einsum(
        "hts,hsj->htj", mixed, value_heads, preferred_element_type=jnp.float32
    ) + lead[:, :, None] * jnp.einsum("hti,hij->htj", query_f, state_in, precision=exact_arithmetic)
    rms = jnp.sqrt(jnp.mean(attn * attn, axis=-1, keepdims=True) + eps_norm)
    normed = attn / rms
    upstream = split_heads(output_gradient, heads).astype(jnp.float32)
    d_attn = (upstream - normed * jnp.mean(upstream * normed, axis=-1, keepdims=True)) / rms
    d_attn_b = d_attn.astype(jnp.bfloat16)
    carried = jnp.einsum(
        "hti,htj->hij", query_f * lead[:, :, None], d_attn, precision=exact_arithmetic
    )
    later = carried_in(
        (gain, carried), "seq", combine, (jnp.ones_like(gain), jnp.zeros_like(carried)), True
    )[1]
    d_mixed = (
        jnp.einsum("htj,hsj->hts", d_attn_b, value_heads, preferred_element_type=jnp.float32)
        * decay_mat
    ).astype(jnp.bfloat16)
    d_query = jnp.einsum(
        "hts,hsi->hti", d_mixed, key_heads, preferred_element_type=jnp.float32
    ) + lead[:, :, None] * jnp.einsum("htj,hij->hti", d_attn, state_in, precision=exact_arithmetic)
    d_value = jnp.einsum(
        "hts,htj->hsj", mixed, d_attn_b, preferred_element_type=jnp.float32
    ) + tail[:, :, None] * jnp.einsum("hsi,hij->hsj", key_f, later, precision=exact_arithmetic)
    sig = jax.nn.sigmoid(query_before_norm)
    query_pre_gradient = join_heads(d_query) * (sig * (1.0 + query_before_norm * (1.0 - sig)))
    value_flat_gradient = join_heads(d_value)
    low_product_float = low_product.astype(jnp.float32)
    up_products = jnp.stack(
        [
            adapter_scale
            * jnp.dot(
                low_product_float[:, :rank_index].T, query_pre_gradient, precision=exact_arithmetic
            ),
            adapter_scale
            * jnp.dot(
                low_product_float[:, rank_index:].T, value_flat_gradient, precision=exact_arithmetic
            ),
        ]
    )
    grad_up = lax.psum(up_products, "seq")
    low_gradient = adapter_scale * jnp.concatenate(
        [
            jnp.dot(
                query_pre_gradient,
                lifting_matrices[0].astype(jnp.float32).T,
                precision=exact_arithmetic,
            ),
            jnp.dot(
                value_flat_gradient,
                lifting_matrices[1].astype(jnp.float32).T,
                precision=exact_arithmetic,
            ),
        ],
        axis=1,
    )
    columns = tokens.astype(jnp.float32)
    grad_down = lax.psum_scatter(
        jnp.dot(columns.T, low_gradient, precision=exact_arithmetic),
        ("seq", "mp"),
        scatter_dimension=0,
        tiled=True,
    )
    return (grad_down, grad_up)


def solution(mesh):
    return jax.shard_map(
        on_device,
        mesh=mesh,
        in_specs=(
            P("seq", None),
            P("seq", "mp"),
            P("seq", "mp"),
            P("seq", "mp"),
            P(),
            P(None, None, "mp"),
            P("mp", "seq"),
            P("seq", "mp"),
        ),
        out_specs=(P(("seq", "mp"), None), P(None, None, "mp")),
        check_vma=False,
    )
```

profile of v0, /device:TPU:2, one launch (start us, length us, event | category | flops | bytes accessed | tf_op | source)
XLA Modules:
  0.0 1261.7 jit_solution(11165250688478119228)
XLA Ops:
  10.7 1.7 convolution_convert_fusion
  12.4 83.2 %all-gather.13.cloned.1.call-done = bf16[3584,1024]{1,0:T(8,128)(2,1)} async-done(((bf16[56,1024]{1,0:T(8,128)(2,1)}), bf16[3584,1024]{1,0:T(8,128)(2,1)}) %all-gather.13.cloned.1.call-update) | async-done | bytes 7340048 | tf_op jit(solution)/shard_map/all_gather | solution.py:69
  95.5 4.2 fusion.57
  100.0 76.9 %all-gather.11.cloned.1.call-done = bf16[3584,1024]{1,0:T(8,128)(2,1)} async-done(((bf16[56,1024]{1,0:T(8,128)(2,1)}), bf16[3584,1024]{1,0:T(8,128)(2,1)}) %all-gather.11.cloned.1.call-update) | async-done | bytes 7340048 | tf_op jit(solution)/shard_map/all_gather | solution.py:68
  176.9 4.3 multiply_convert_fusion
  181.2 1.5 fusion.16
  184.2 127.0 %all-reduce = f32[512]{0:T(512)S(1)} all-reduce(f32[512]{0:T(512)S(1)} %dynamic-update-slice), channel_id=2, replica_groups=mesh['seq'=64,'mp'=4] {'seq'}, use_global_device_ids=true, to_apply=%add | all-reduce | flops 512 | bytes 4096
  313.5 4.3 fusion.56
  317.8 1.2 multiply_convert_fusion.1
  320.1 1.8 fusion.9
  321.8 78.4 %all-gather.15.cloned.1.call-done = f32[512,128,128]{2,1,0:T(8,128)} async-done(((f32[8,128,128]{2,1,0:T(8,128)}), f32[512,128,128]{2,1,0:T(8,128)}) %all-gather.15.cloned.1.call-update) | async-done | bytes 33554448 | tf_op jit(solution)/shard_map/all_gather | solution.py:13
  400.3 118.5 %while.28 = (s32[]{:T(128)}, f32[8,128,128]{2,1,0:T(8,128)S(1)}, s32[]{:T(128)}, f32[64,8]{1,0:T(8,128)}, f32[64,8,128,128]{3,2,1,0:T(8,128)}, /*index=5*/s32[]{:T(128)}, s32[]{:T(128)}) while((s32[]{:T(128)}, f32[8,128,128]{2,1,0:T(8,128)S(1)}, s32[]{:T(128)}, f32[64,8]{1,0:T(8,128)}, f32[64,8,128,128]{3,2,1,0:T(8,128)}, ...), condition=%wide.region_2.3_spmd.clone, body=%wide.region_1.2_spmd.clone.sunk | while | flops 524292 | bytes 1573073 | solution.py:25
  400.9 1.2 fusion.87
  402.8 1.2 fusion.87
  404.7 1.2 fusion.87
  406.6 1.2 fusion.87
  408.5 1.2 fusion.87
  410.3 1.2 fusion.87
  412.2 1.2 fusion.87
  414.1 1.2 fusion.87
  416.0 1.2 fusion.87
  417.9 1.2 fusion.87
  419.8 1.2 fusion.87
  421.6 1.2 fusion.87
  423.5 1.2 fusion.87
  425.4 1.2 fusion.87
  427.3 1.2 fusion.87
  429.2 1.2 fusion.87
  438.6 1.2 fusion.87
  463.1 1.2 fusion.87
  513.8 1.2 fusion.87
  519.4 1.4 multiply_reduce_fusion.1
  520.9 2.0 fusion.13
  523.2 1.4 rev.6
  526.2 1.3 fusion.2
  527.6 1.2 multiply_multiply_fusion
  528.9 1.3 fusion.36
  530.2 131.7 %all-gather.17.cloned.1.call-done = f32[512,128,128]{2,1,0:T(8,128)} async-done(((f32[8,128,128]{2,1,0:T(8,128)}), f32[512,128,128]{2,1,0:T(8,128)}) %all-gather.17.cloned.1.call-update) | async-done | bytes 33554448 | tf_op jit(solution)/shard_map/all_gather | solution.py:13
  661.9 23.0 %rev.7 = f32[64,8,128,128]{3,2,1,0:T(8,128)} reverse(f32[64,8,128,128]{3,2,1,0:T(8,128)} %bitcast.144), dimensions={0} | reverse | bytes 67108864 | tf_op jit(solution)/shard_map/rev | solution.py:15
  684.9 118.6 %while.29 = (s32[]{:T(128)}, f32[8,128,128]{2,1,0:T(8,128)S(1)}, s32[]{:T(128)}, f32[64,8]{1,0:T(8,128)}, f32[64,8,128,128]{3,2,1,0:T(8,128)}, /*index=5*/s32[]{:T(128)}, s32[]{:T(128)}) while((s32[]{:T(128)}, f32[8,128,128]{2,1,0:T(8,128)S(1)}, s32[]{:T(128)}, f32[64,8]{1,0:T(8,128)}, f32[64,8,128,128]{3,2,1,0:T(8,128)}, ...), condition=%wide.region_6.7_spmd.clone, body=%wide.region_5.6_spmd.clone.sunk | while | flops 524292 | bytes 1573073 | solution.py:25
  698.8 1.2 fusion.88
  719.5 1.2 fusion.88
  768.5 1.2 fusion.88
  791.0 1.2 fusion.88
  804.6 2.1 convolution_bitcast_fusion
  808.5 258.2 %all-reduce.7.cloned.1.call-done = f32[3584,128]{0,1:T(8,128)} async-done(((f32[3584,128]{0,1:T(8,128)}), f32[3584,128]{0,1:T(8,128)}) %all-reduce.7.cloned.1.call-update) | async-done | bytes 1835024
  1068.3 184.6 %all-reduce.5.cloned.1.call-done = f32[2,64,1024]{2,1,0:T(8,128)} async-done(((f32[2,64,1024]{2,1,0:T(8,128)}), f32[2,64,1024]{2,1,0:T(8,128)}) %all-reduce.5.cloned.1.call-update) | async-done | bytes 524304 | tf_op jit(solution)/shard_map/psum | solution.py:138
  1252.9 1.9 copy.120
  (294 shorter events, 222.1 us)
Async XLA Ops:
  7.2 3.5 copy-start
  7.2 88.4 %all-gather.13.cloned.1.call-start = ((), (), s32[]{:S(2)}) async-start(), calls=%async_computation.2 | async-start | bytes 7454720 | tf_op jit(solution)/shard_map/all_gather | solution.py:69
  7.9 169.0 %all-gather.11.cloned.1.call-start = ((), (), s32[]{:S(2)}) async-start(), calls=%async_computation.1 | async-start | bytes 7454720 | tf_op jit(solution)/shard_map/all_gather | solution.py:68
  8.7 304.8 %all-gather.9.cloned.1.call-start = ((), (), s32[]{:S(2)}) async-start(), calls=%async_computation | async-start | bytes 7454720 | tf_op jit(solution)/shard_map/all_gather | solution.py:67
  9.4 390.9 %all-gather.15.cloned.1.call-start = ((), (), s32[]{:S(2)}) async-start(), calls=%async_computation.4 | async-start | bytes 34078720 | tf_op jit(solution)/shard_map/all_gather | solution.py:13
  12.4 305.4 %copy-start.7 = (bf16[128,128]{0,1:T(8,128)(2,1)}, bf16[128,128]{0,1:T(8,128)(2,1)S(1)}, u32[]{:S(2)}) copy-start(bf16[128,128]{0,1:T(8,128)(2,1)S(1)} %convolution_convert_fusion) | copy-start | bytes 98308
  12.4 87.4 %copy-start.4 = (bf16[2,64,1024]{2,1,0:T(8,128)(2,1)S(1)}, bf16[2,64,1024]{2,1,0:T(8,128)(2,1)}, u32[]{:S(2)}) copy-start(bf16[2,64,1024]{2,1,0:T(8,128)(2,1)} %param.17) | copy-start | bytes 786436
  100.0 82.8 %copy-start.9 = (u32[256]{0:T(256)S(1)}, u32[256]{0:T(256)}, u32[]{:S(2)}) copy-start(u32[256]{0:T(256)} %constant.80) | copy-start | bytes 3076
  100.0 212.0 %copy-start.6 = (bf16[128,1024]{1,0:T(8,128)(2,1)S(1)}, bf16[128,1024]{1,0:T(8,128)(2,1)}, u32[]{:S(2)}) copy-start(bf16[128,1024]{1,0:T(8,128)(2,1)} %param.19) | copy-start | bytes 786436
  181.2 138.9 %copy-start.1 = (bf16[128,1024]{1,0:T(8,128)(2,1)}, bf16[128,1024]{1,0:T(8,128)(2,1)S(1)}, u32[]{:S(2)}) copy-start(bf16[128,1024]{1,0:T(8,128)(2,1)S(1)} %multiply_convert_fusion) | copy-start | bytes 786436
  182.8 479.1 %all-gather.17.cloned.1.call-start = ((), (), s32[]{:S(2)}) async-start(), calls=%async_computation.5 | async-start | bytes 34078720 | tf_op jit(solution)/shard_map/all_gather | solution.py:13
  522.9 543.7 %all-reduce.7.cloned.1.call-start = ((), (), s32[]{:S(2)}) async-start(), calls=%async_computation.6 | async-start | bytes 3670016
  684.9 118.6 %copy-start.2 = (bf16[128,1024]{1,0:T(8,128)(2,1)S(1)}, bf16[128,1024]{1,0:T(8,128)(2,1)}, u32[]{:S(2)}) copy-start(bf16[128,1024]{1,0:T(8,128)(2,1)} %copy-done.1) | copy-start | bytes 786436
  684.9 119.2 %copy-start.3 = (bf16[8,128,128]{2,1,0:T(8,128)(2,1)S(1)}, bf16[8,128,128]{2,1,0:T(8,128)(2,1)}, u32[]{:S(2)}) copy-start(bf16[8,128,128]{2,1,0:T(8,128)(2,1)} %fusion.9) | copy-start | bytes 786436
  684.9 119.4 %copy-start.5 = (bf16[2,64,1024]{2,1,0:T(8,128)(2,1)S(1)}, bf16[2,64,1024]{2,1,0:T(8,128)(2,1)}, u32[]{:S(2)}) copy-start(bf16[2,64,1024]{2,1,0:T(8,128)(2,1)} %param.17) | copy-start | bytes 786436
  684.9 121.9 %copy-start.8 = (bf16[128,128]{0,1:T(8,128)(2,1)S(1)}, bf16[128,128]{0,1:T(8,128)(2,1)}, u32[]{:S(2)}) copy-start(bf16[128,128]{0,1:T(8,128)(2,1)} %copy-done.7) | copy-start | bytes 98308
  806.8 446.2 %all-reduce.5.cloned.1.call-start = ((), (), s32[]{:S(2)}) async-start(), calls=%async_computation.3 | async-start | bytes 1048576 | tf_op jit(solution)/shard_map/psum | solution.py:138
Sparse Core Ops, SparseCore 0:
  10.7 84.7 all-gather.12
  98.3 78.5 all-gather.10
  179.7 78.6 all-gather.8
  261.6 138.6 all-gather.14
  523.1 138.7 all-gather.16
  806.9 259.7 all-reduce.6
  1070.7 182.1 all-reduce.4
where the time goes:
time: 1270 us; the launch traced here: 1260 us
  waiting for transfers between devices  815 us (64%)
  other arithmetic  151 us (12%)
  blocking collectives  127 us (10%)
  local copies, waits for them, and re-layouts  119 us (9%)
  matrix products  30.3 us (2%)
  between operations  15 us (1%)
    unnamed x8, waiting for transfers between devices  260 us
    all_gather x2, waiting for transfers between devices, carried_in(): pieces = jax.tree.map(lambda part: lax.all_gather(part, axis), value)  210 us
    psum x1, waiting for transfers between devices, on_device(): grad_up = lax.psum(up_products, 'seq')  185 us
    select_n x126, other arithmetic, hop(): jnp.where(position < mine, new, old)  147 us
    unnamed x1, blocking collectives  127 us
    mul x126, local copies, waits for them, and re-layouts, combine(): later[0][:, None, None] * earlier[1] + later[1]  86.6 us
    all_gather x1, waiting for transfers between devices, on_device(): lax.all_gather(value_weight, 'seq', axis=0, tiled=True)  83.2 us
    all_gather x1, waiting for transfers between devices, on_device(): lax.all_gather(key_weight, 'seq', axis=0, tiled=True)  76.9 us
  transfers between devices with their start and end apart: 7, of which 6 were waited for; matrix products, arithmetic and copies ran while one was open for 3% of the time, Pallas kernels for 0%

commit v1 on v0

--- a/solution.py
+++ b/solution.py
@@ -6,6 +6,13 @@
 adapter_scale = 2.0
 eps_norm = 1e-06
 exact_arithmetic = lax.Precision.HIGHEST
+
+
+def all_by_exchange(x, axis, dim):
+    peers = lax.axis_size(axis)
+    blocks = jnp.stack([x for _ in range(peers)])
+    blocks = lax.all_to_all(blocks, axis, split_axis=0, concat_axis=0)
+    return jnp.concatenate(blocks, axis=dim)
 
 
 def carried_in(value, axis, join, neutral, backward):
@@ -66,7 +73,7 @@
     pieces = (
         lax.all_gather(query_weight, "seq", axis=0, tiled=True),
         lax.all_gather(key_weight, "seq", axis=0, tiled=True),
-        lax.all_gather(value_weight, "seq", axis=0, tiled=True),
+        all_by_exchange(value_weight, "seq", 0),
     )
     columns = tokens
     query_frozen_part, key_base, value_frozen_part = tuple(

time: 1270 us -> 1250 us (0.984)
  waiting for transfers between devices: 815 us -> 777 us
    all_to_all x0 -> x1, waiting for transfers between devices: none -> 189 us  [all_by_exchange(): blocks = lax.all_to_all(blocks, axis, split_axis=0, concat_axis=0)]
    all_gather x1 -> x0, waiting for transfers between devices: 83.2 us -> none  [on_device(): lax.all_gather(value_weight, 'seq', axis=0, tiled=True)]
    all_gather x1, waiting for transfers between devices: 76.9 us -> 0.02 us  [on_device(): lax.all_gather(key_weight, 'seq', axis=0, tiled=True)]
    all_gather x2, waiting for transfers between devices: 210 us -> 144 us  [carried_in(): pieces = jax.tree.map(lambda part: lax.all_gather(part, axis), value)]
    unnamed x8 -> x7, waiting for transfers between devices: 260 us -> 260 us
  transfers between devices with their start and end apart: 7 -> 7, of which waited for: 6 -> 5; matrix products, arithmetic and copies ran while one was open for 3% -> 3% of each run, Pallas kernels for 0% -> 0%
where the time goes in v1:
time: 1250 us; the launch traced here: 1240 us
  waiting for transfers between devices  777 us (62%)
  other arithmetic  150 us (12%)
  blocking collectives  130 us (10%)
  local copies, waits for them, and re-layouts  124 us (10%)
  matrix products  29.5 us (2%)
  between operations  15.1 us (1%)
  starting transfers between devices  12.9 us (1%)
    unnamed x7, waiting for transfers between devices  260 us
    all_to_all x1, waiting for transfers between devices, all_by_exchange(): blocks = lax.all_to_all(blocks, axis, split_axis=0, concat_axis=0)  189 us
    psum x1, waiting for transfers between devices, on_device(): grad_up = lax.psum(up_products, 'seq')  184 us
    select_n x126, other arithmetic, hop(): jnp.where(position < mine, new, old)  147 us
    all_gather x2, waiting for transfers between devices, carried_in(): pieces = jax.tree.map(lambda part: lax.all_gather(part, axis), value)  144 us
    unnamed x1, blocking collectives  130 us
    mul x126, local copies, waits for them, and re-layouts, combine(): later[0][:, None, None] * earlier[1] + later[1]  86.6 us
  transfers between devices with their start and end apart: 7, of which 5 were waited for; matrix products, arithmetic and copies ran while one was open for 3% of the time, Pallas kernels for 0%

profile of v1, /device:TPU:2, one launch (start us, length us, event | category | flops | bytes accessed | tf_op | source)
XLA Modules:
  0.0 1241.8 jit_solution(1314748465940290323)
XLA Ops:
  7.9 4.8 stack.8
  12.7 12.5 %all-to-all-start = ((bf16[64,56,1024]{2,1,0:T(8,128)(2,1)}), bf16[64,56,1024]{2,1,0:T(8,128)(2,1)}, u32[]{:S(2)}, u32[]{:S(2)}) async-start(bf16[64,56,1024]{2,1,0:T(8,128)(2,1)} %stack.8), calls=%async_computation | async-start | bytes 14680064 | tf_op jit(solution)/shard_map/all_to_all | solution.py:14
  27.0 188.9 %all-to-all-done = bf16[64,56,1024]{2,1,0:T(8,128)(2,1)} async-done(((bf16[64,56,1024]{2,1,0:T(8,128)(2,1)}), bf16[64,56,1024]{2,1,0:T(8,128)(2,1)}, u32[]{:S(2)}, u32[]{:S(2)}) %all-to-all-start) | async-done | bytes 7340064 | tf_op jit(solution)/shard_map/all_to_all | solution.py:14
  215.9 4.3 fusion.57
  220.6 4.5 multiply_convert_fusion
  225.1 1.5 fusion.16
  228.3 130.4 %all-reduce = f32[512]{0:T(512)S(1)} all-reduce(f32[512]{0:T(512)S(1)} %dynamic-update-slice), channel_id=2, replica_groups=mesh['seq'=64,'mp'=4] {'seq'}, use_global_device_ids=true, to_apply=%add | all-reduce | flops 512 | bytes 4096
  360.1 4.2 fusion.56
  364.3 1.2 multiply_convert_fusion.1
  367.4 1.8 fusion.9
  369.2 12.3 all-gather.12.cloned.1.call-done
  381.5 118.0 %while.28 = (s32[]{:T(128)}, f32[8,128,128]{2,1,0:T(8,128)S(1)}, s32[]{:T(128)}, f32[64,8]{1,0:T(8,128)}, f32[64,8,128,128]{3,2,1,0:T(8,128)}, /*index=5*/s32[]{:T(128)}, s32[]{:T(128)}) while((s32[]{:T(128)}, f32[8,128,128]{2,1,0:T(8,128)S(1)}, s32[]{:T(128)}, f32[64,8]{1,0:T(8,128)}, f32[64,8,128,128]{3,2,1,0:T(8,128)}, ...), condition=%wide.region_2.3_spmd.clone, body=%wide.region_1.2_spmd.clone.sunk | while | flops 524292 | bytes 1573065 | solution.py:32
  382.2 1.2 fusion.87
  384.1 1.2 fusion.87
  386.0 1.2 fusion.87
  387.8 1.2 fusion.87
  389.7 1.2 fusion.87
  391.6 1.2 fusion.87
  393.4 1.2 fusion.87
  395.3 1.2 fusion.87
  397.2 1.2 fusion.87
  399.1 1.2 fusion.87
  400.9 1.2 fusion.87
  402.8 1.2 fusion.87
  404.7 1.2 fusion.87
  406.6 1.2 fusion.87
  408.4 1.2 fusion.87
  410.3 1.2 fusion.87
  412.2 1.2 fusion.87
  414.1 1.2 fusion.87
  434.6 1.2 fusion.87
  445.9 1.2 fusion.87
  457.1 1.2 fusion.87
  500.1 1.4 multiply_reduce_fusion.1
  501.7 2.0 fusion.13
  503.9 1.4 rev.6
  506.9 1.3 fusion.2
  508.4 1.2 multiply_multiply_fusion
  509.7 1.3 fusion.36
  511.0 131.6 %all-gather.14.cloned.1.call-done = f32[512,128,128]{2,1,0:T(8,128)} async-done(((f32[8,128,128]{2,1,0:T(8,128)}), f32[512,128,128]{2,1,0:T(8,128)}) %all-gather.14.cloned.1.call-update) | async-done | bytes 33554448 | tf_op jit(solution)/shard_map/all_gather | solution.py:20
  642.6 23.0 %rev.7 = f32[64,8,128,128]{3,2,1,0:T(8,128)} reverse(f32[64,8,128,128]{3,2,1,0:T(8,128)} %bitcast.145), dimensions={0} | reverse | bytes 67108864 | tf_op jit(solution)/shard_map/rev | solution.py:22
  665.6 118.2 %while.29 = (s32[]{:T(128)}, f32[8,128,128]{2,1,0:T(8,128)S(1)}, s32[]{:T(128)}, f32[64,8]{1,0:T(8,128)}, f32[64,8,128,128]{3,2,1,0:T(8,128)}, /*index=5*/s32[]{:T(128)}, s32[]{:T(128)}) while((s32[]{:T(128)}, f32[8,128,128]{2,1,0:T(8,128)S(1)}, s32[]{:T(128)}, f32[64,8]{1,0:T(8,128)}, f32[64,8,128,128]{3,2,1,0:T(8,128)}, ...), condition=%wide.region_6.7_spmd.clone, body=%wide.region_5.6_spmd.clone.sunk | while | flops 524292 | bytes 1573065 | solution.py:32
  750.7 1.2 fusion.88
  769.5 1.2 fusion.88
  784.9 2.1 convolution_bitcast_fusion
  788.7 258.2 %all-reduce.7.cloned.1.call-done = f32[3584,128]{0,1:T(8,128)} async-done(((f32[3584,128]{0,1:T(8,128)}), f32[3584,128]{0,1:T(8,128)}) %all-reduce.7.cloned.1.call-update) | async-done | bytes 1835024
  1048.6 184.4 %all-reduce.5.cloned.1.call-done = f32[2,64,1024]{2,1,0:T(8,128)} async-done(((f32[2,64,1024]{2,1,0:T(8,128)}), f32[2,64,1024]{2,1,0:T(8,128)}) %all-reduce.5.cloned.1.call-update) | async-done | bytes 524304 | tf_op jit(solution)/shard_map/psum | solution.py:145
  1233.1 1.9 copy.120
  (298 shorter events, 221.3 us)
Async XLA Ops:
  7.2 19.4 %copy-start = (bf16[128,3584]{1,0:T(8,128)(2,1)S(1)}, bf16[128,3584]{1,0:T(8,128)(2,1)}, u32[]{:S(2)}) copy-start(bf16[128,3584]{1,0:T(8,128)(2,1)} %param.12) | copy-start | bytes 2752516
  7.2 213.4 %all-gather.10.cloned.1.call-start = ((), (), s32[]{:S(2)}) async-start(), calls=%async_computation.2 | async-start | bytes 7454720 | tf_op jit(solution)/shard_map/all_gather | solution.py:75
  12.7 13.3 %copy-start.10 = (f32[8,128]{1,0:T(8,128)S(1)}, f32[8,128]{1,0:T(8,128)}, u32[]{:S(2)}) copy-start(f32[8,128]{1,0:T(8,128)} %param.18) | copy-start | bytes 12292
  12.7 13.8 %copy-start.4 = (bf16[3584,128]{1,0:T(8,128)(2,1)S(1)}, bf16[3584,128]{1,0:T(8,128)(2,1)}, u32[]{:S(2)}) copy-start(bf16[3584,128]{1,0:T(8,128)(2,1)} %param.16) | copy-start | bytes 2752516
  12.7 203.3 %all-to-all-start = ((bf16[64,56,1024]{2,1,0:T(8,128)(2,1)}), bf16[64,56,1024]{2,1,0:T(8,128)(2,1)}, u32[]{:S(2)}, u32[]{:S(2)}) async-start(bf16[64,56,1024]{2,1,0:T(8,128)(2,1)} %stack.8), calls=%async_computation | async-start | bytes 14680064 | tf_op jit(solution)/shard_map/all_to_all | solution.py:14
  25.2 334.9 %all-gather.8.cloned.1.call-start = ((), (), s32[]{:S(2)}) async-start(), calls=%async_computation.1 | async-start | bytes 7454720 | tf_op jit(solution)/shard_map/all_gather | solution.py:74
  25.9 355.6 %all-gather.12.cloned.1.call-start = ((), (), s32[]{:S(2)}) async-start(), calls=%async_computation.4 | async-start | bytes 34078720 | tf_op jit(solution)/shard_map/all_gather | solution.py:20
  27.0 337.3 %copy-start.8 = (bf16[128,128]{0,1:T(8,128)(2,1)}, bf16[128,128]{0,1:T(8,128)(2,1)S(1)}, u32[]{:S(2)}) copy-start(bf16[128,128]{0,1:T(8,128)(2,1)S(1)} %convolution_convert_fusion) | copy-start | bytes 98308
  215.9 4.3 copy-start.5
  220.5 6.3 copy-start.11
  220.5 138.8 %copy-start.7 = (bf16[128,1024]{1,0:T(8,128)(2,1)S(1)}, bf16[128,1024]{1,0:T(8,128)(2,1)}, u32[]{:S(2)}) copy-start(bf16[128,1024]{1,0:T(8,128)(2,1)} %param.19) | copy-start | bytes 786436
  225.1 142.3 %copy-start.1 = (bf16[128,1024]{1,0:T(8,128)(2,1)}, bf16[128,1024]{1,0:T(8,128)(2,1)S(1)}, u32[]{:S(2)}) copy-start(bf16[128,1024]{1,0:T(8,128)(2,1)S(1)} %multiply_convert_fusion) | copy-start | bytes 786436
  226.7 415.9 %all-gather.14.cloned.1.call-start = ((), (), s32[]{:S(2)}) async-start(), calls=%async_computation.5 | async-start | bytes 34078720 | tf_op jit(solution)/shard_map/all_gather | solution.py:20
  503.7 543.3 %all-reduce.7.cloned.1.call-start = ((), (), s32[]{:S(2)}) async-start(), calls=%async_computation.6 | async-start | bytes 3670016
  665.6 118.2 %copy-start.2 = (bf16[128,1024]{1,0:T(8,128)(2,1)S(1)}, bf16[128,1024]{1,0:T(8,128)(2,1)}, u32[]{:S(2)}) copy-start(bf16[128,1024]{1,0:T(8,128)(2,1)} %copy-done.1) | copy-start | bytes 786436
  665.6 118.8 %copy-start.3 = (bf16[8,128,128]{2,1,0:T(8,128)(2,1)S(1)}, bf16[8,128,128]{2,1,0:T(8,128)(2,1)}, u32[]{:S(2)}) copy-start(bf16[8,128,128]{2,1,0:T(8,128)(2,1)} %fusion.9) | copy-start | bytes 786436
  665.6 119.0 %copy-start.6 = (bf16[2,64,1024]{2,1,0:T(8,128)(2,1)S(1)}, bf16[2,64,1024]{2,1,0:T(8,128)(2,1)}, u32[]{:S(2)}) copy-start(bf16[2,64,1024]{2,1,0:T(8,128)(2,1)} %param.17) | copy-start | bytes 786436
  665.6 121.6 %copy-start.9 = (bf16[128,128]{0,1:T(8,128)(2,1)S(1)}, bf16[128,128]{0,1:T(8,128)(2,1)}, u32[]{:S(2)}) copy-start(bf16[128,128]{0,1:T(8,128)(2,1)} %copy-done.8) | copy-start | bytes 98308
  787.1 446.0 %all-reduce.5.cloned.1.call-start = ((), (), s32[]{:S(2)}) async-start(), calls=%async_computation.3 | async-start | bytes 1048576 | tf_op jit(solution)/shard_map/psum | solution.py:145
Sparse Core Ops, SparseCore 0:
  10.7 127.7 all-gather.9
  141.3 96.0 all-gather.7
  240.7 140.8 all-gather.11
  503.8 138.7 all-gather.13
  787.2 259.7 all-reduce.6
  1050.9 182.1 all-reduce.4
